TPU v7x, 256 devices: a whole 4x4x8 slice. The times are simulated.
256 devices in a mesh: inst: 8 (over y_hi, x), space: 32 (over z, y_lo, core).
Axes of the slice: x: 4, y: 4 (y_hi: 2, y_lo: 2; y = y_hi * 2 + y_lo), z: 8, core: 2. Of those that a mesh axis runs over, the one named last changes fastest.
Arguments:
- psi_start: float32 [5, 8, 256, 1024], P(None, 'inst', 'space'), may hold values from -6 to 6
- density: float32 [8, 256, 1024], P('inst', 'space'), may hold values from 0.8 to 1.25
- velocity: float32 [3, 8, 256, 1024], P(None, 'inst', 'space'), may hold values from -0.6 to 0.6
- pressure: float32 [8, 256, 1024], P('inst', 'space'), may hold values from 0.5 to 1
- obs_pos: float32 [3, 512], P(None, 'space'), may hold values from -16 to 16, as said below
- obs_weight: float32 [2, 512], P(None, 'space'), may hold values from -0.6 to 0.6
- obs_harmonic: int32 [512], P('space'), may hold values from 1 to 3
- panel_pos: float32 [3, 65536], replicated, may hold values from -1 to 1
- panel_normal: float32 [3, 65536], P(None, 'space'), may hold values from -5 to 5
- panel_cell: int32 [65536], P('space'), may hold values from 0 to 8191
- plane_nbr: int32 [4, 1024], replicated, may hold values from 0 to 1023
Outputs:
- adjoint: float32 [5, 8, 256, 1024], P(None, 'inst', 'space')
Inputs may be any that keep to these rules, and one draw needn't show every extreme that they name: `obs_pos`: observers lie between 8 and 16 from the anchor, outside the panels' cube. panel_cell[q] is an index into the 8 x 1024 cells of the slot's owner, layer panel_cell[q] // 1024.
All inputs are finite; a program needn't handle non-finite values.
Results may differ from a plain program's by a relative error of at most 0.0001.
Values sent between devices are 32-bit elements; how exact they have to be, the bound alone decides.
A program may use at most 64 MiB of HBM per device.

v0:
```python
import math

import jax
import jax.numpy as jnp
from jax import lax
from jax.sharding import PartitionSpec as P

ITERS = 3


GAMMA = 1.4
KWAVE = 0.7
RADIUS = 10.0
TAU = 0.05
DISSIP = 0.25
OMEGA = 1.5
VISCO = 0.5


def padded_2(cells, sides, width):
    for axis, dim in sides:
        count = lax.axis_size(axis)
        head = lax.slice_in_dim(cells, 0, width, axis=dim)
        tail = lax.slice_in_dim(cells, cells.shape[dim] - width, cells.shape[dim], axis=dim)
        cells = jnp.concatenate(
            [
                lax.ppermute(tail, axis, [(i, (i + 1) % count) for i in range(count)]),
                cells,
                lax.ppermute(head, axis, [((i + 1) % count, i) for i in range(count)]),
            ],
            axis=dim,
        )
    return cells


def panel_block(observers, panels, time_now):
    delta = panels[:, None, :] - observers[:3, :, None]
    dist2 = jnp.sum(delta * delta, axis=0)
    dist = jnp.sqrt(dist2)
    harm = observers[5][:, None]
    phase = harm * (time_now - KWAVE * dist)
    amp = (
        (observers[3][:, None] * jnp.cos(phase) + observers[4][:, None] * jnp.sin(phase))
        * (RADIUS * RADIUS)
        / (dist2 * dist)
    )
    return jnp.sum(amp[None] * delta, axis=1)


def sensitivity(observers, panels, time_now):
    count = panels.shape[1]
    obs_count = observers.shape[1]
    block = math.gcd(count, max(128, 262144 // obs_count))
    split = panels.reshape(3, count // block, block).transpose(1, 0, 2)
    out = lax.map(lambda piece: panel_block(observers, piece, time_now), split)
    return out.transpose(1, 0, 2).reshape(3, count)


def conserved(density, velocity, pressure):
    moment = density[None] * velocity
    energy = pressure / (GAMMA - 1.0) + 0.5 * density * jnp.sum(velocity * velocity, axis=0)
    return jnp.concatenate([density[None], moment, energy[None]], axis=0)


def fluxes(state):
    dens = state[0]
    moment = state[1:4]
    energy = state[4]
    vel = moment / dens
    press = (GAMMA - 1.0) * (energy - 0.5 * jnp.sum(moment * vel, axis=0))
    result = []
    for axis_d in range(3):
        comps = [moment[axis_d]]
        for axis_e in range(3):
            term = moment[axis_e] * vel[axis_d]
            if axis_e == axis_d:
                term = term + press
            comps.append(term)
        comps.append((energy + press) * vel[axis_d])
        result.append(jnp.stack(comps))
    return tuple(result)


def spectral_coeff(offset, count):
    safe = jnp.where(offset == 0, 1.0, offset)
    angle = math.pi * safe / count
    even_odd_flag = 1.0 - 2.0 * jnp.mod(safe, 2.0)
    other = (
        -(OMEGA / 2.0) * even_odd_flag * jnp.cos(angle) / jnp.sin(angle)
        + VISCO * (OMEGA * OMEGA / 2.0) * even_odd_flag / jnp.sin(angle) ** 2
    )
    return jnp.where(offset == 0, VISCO * OMEGA * OMEGA * (count * count + 2.0) / 12.0, other)


def shards(
    psi_start,
    density,
    velocity,
    pressure,
    obs_pos,
    obs_weight,
    obs_harmonic,
    panel_pos,
    panel_normal,
    panel_cell,
    plane_nbr,
):
    inst_count = lax.axis_size("inst")
    inst_id = lax.axis_index("inst")
    space_id = lax.axis_index("space")
    time_now = 2.0 * math.pi * inst_id.astype(jnp.float32) / inst_count
    observers = jnp.concatenate(
        [obs_pos, obs_weight, obs_harmonic[None].astype(jnp.float32)], axis=0
    )
    owned_count = panel_normal.shape[1]
    whole = sensitivity(observers, panel_pos, time_now)
    total = lax.psum(whole, "space")
    sens = lax.dynamic_slice_in_dim(total, space_id * owned_count, owned_count, 1)
    weight = jnp.sum(sens * panel_normal, axis=0)
    layers = psi_start.shape[2]
    plane = psi_start.shape[3]
    wall = jax.ops.segment_sum(weight, panel_cell, num_segments=layers * plane).reshape(
        layers, plane
    )
    dens = density[0]
    vel = velocity[:, 0]
    state = conserved(dens, vel, pressure[0])
    slope = jnp.concatenate(
        [0.5 * jnp.sum(vel * vel, axis=0)[None], -vel, jnp.ones_like(dens)[None]], axis=0
    ) * (GAMMA - 1.0)
    source = slope * wall[None]
    _, pull = jax.vjp(fluxes, state)
    psi = psi_start[:, 0]
    for step in range(ITERS):
        padded = padded_2(psi, (("space", 1),), 1)
        minus_a = padded[:, :-2]
        plus_a = padded[:, 2:]
        plus_y = jnp.take(psi, plane_nbr[0], axis=2)
        minus_y = jnp.take(psi, plane_nbr[1], axis=2)
        plus_z = jnp.take(psi, plane_nbr[2], axis=2)
        minus_z = jnp.take(psi, plane_nbr[3], axis=2)
        middle_point = pull(
            (0.5 * (minus_a - plus_a), 0.5 * (minus_y - plus_y), 0.5 * (minus_z - plus_z))
        )[0]
        spread = 6.0 * psi - (minus_a + plus_a + plus_y + minus_y + plus_z + minus_z)
        every_instant = lax.all_gather(psi[:, None], "inst", axis=1, tiled=True)
        others = jnp.arange(inst_count, dtype=jnp.int32)
        row_entry = spectral_coeff(
            jnp.mod(inst_id - others, inst_count).astype(jnp.float32), float(inst_count)
        )
        spectral_operator = jnp.einsum(
            "c,kcyo->kyo", row_entry, every_instant, precision=lax.Precision.HIGHEST
        )
        psi = psi - TAU * (middle_point + DISSIP * spread + spectral_operator + source)
    return psi[:, None]


def solution(mesh):
    placed = (
        P(None, "inst", "space", None),
        P("inst", "space", None),
        P(None, "inst", "space", None),
        P("inst", "space", None),
        P(None, "space"),
        P(None, "space"),
        P("space"),
        P(),
        P(None, "space"),
        P("space"),
        P(),
    )
    return jax.shard_map(
        shards,
        mesh=mesh,
        in_specs=placed,
        out_specs=P(None, "inst", "space", None),
        check_vma=False,
    )
```

profile of v0, /device:TPU:1, one launch (start us, length us, event | category | flops | bytes accessed | tf_op | source)
XLA Modules:
  0.0 504.6 jit_solution(14409982304165432410)
XLA Ops:
  8.0 38.1 %while.10 = (s32[]{:T(128)}, f32[4,3,16384]{2,1,0:T(4,128)}, f32[2,16]{1,0:T(2,128)}, f32[1,16]{1,0:T(1,128)S(1)}, f32[]{:T(128)}, /*index=5*/f32[4,3,16384]{2,1,0:T(4,128)}, f32[3,16]{1,0:T(4,128)}, s32[]{:T(128)}) while((s32[]{:T(128)}, f32[4,3,16384]{2,1,0:T(4,128)}, f32[2,16]{1,0:T(2,128)}, f32[1,16]{1,0:T(1,128)S(1)}, f32[]{:T(128)}, ...), condition=%wide.region_6.8_spmd, body=%wide.region_3.7_spmd.sunk | while | flops 6766594 | bytes 5637533 | solution.py:55
  11.1 4.3 fusion.108
  20.6 4.3 fusion.108
  30.1 4.3 fusion.108
  39.6 4.3 fusion.108
  47.3 2.8 collective-permute-start
  53.4 10.4 %gather_fusion = f32[1024,5,8]{2,1,0:T(8,128)} fusion(f32[5,8,1024]{1,0,2:T(8,128)} %copy.184, s32[1024]{0:T(1024)S(1)} %fusion.60), kind=kCustom, calls=%fused_computation.clone | custom fusion | bytes 331776 | tf_op jit(solution)/shard_map/jit(_take)/gather | solution.py:141
  66.4 10.5 %gather_fusion.1 = f32[1024,5,8]{2,1,0:T(8,128)} fusion(f32[5,8,1024]{1,0,2:T(8,128)} %copy.184, s32[1024]{0:T(1024)S(1)} %fusion.61), kind=kCustom, calls=%fused_computation.1.clone | custom fusion | bytes 331776 | tf_op jit(solution)/shard_map/jit(_take)/gather | solution.py:140
  79.5 10.4 %gather_fusion.2 = f32[1024,5,8]{2,1,0:T(8,128)} fusion(f32[5,8,1024]{1,0,2:T(8,128)} %copy.184, s32[1024]{0:T(1024)S(1)} %fusion.62), kind=kCustom, calls=%fused_computation.2.clone | custom fusion | bytes 331776 | tf_op jit(solution)/shard_map/jit(_take)/gather | solution.py:139
  89.9 2.8 copy.189
  92.7 10.4 %gather_fusion.3 = f32[1024,5,8]{2,1,0:T(8,128)} fusion(f32[5,8,1024]{1,0,2:T(8,128)} %copy.184, s32[1024]{0:T(1024)S(1)} %fusion.63), kind=kCustom, calls=%fused_computation.3.clone | custom fusion | bytes 331776 | tf_op jit(solution)/shard_map/jit(_take)/gather | solution.py:138
  103.0 2.6 copy.191
  106.2 173.2 %all-reduce.80.cloned.1.call-done = f32[3,65536]{1,0:T(4,128)} async-done(((f32[3,65536]{1,0:T(4,128)}), f32[3,65536]{1,0:T(4,128)}) %all-reduce.80.cloned.1.call-update) | async-done | bytes 786448 | tf_op jit(solution)/shard_map/psum | solution.py:117
  280.3 11.6 %scatter_custom_fusion = f32[8192]{0:T(1024)S(1)} fusion(s32[2048]{0:T(1024)} %param.24, f32[2048]{0:T(1024)S(1)} %multiply_reduce_fusion.4, f32[]{:T(128)} %constant.59.clone.1), kind=kCustom, calls=%fused_computation.205 | custom fusion | flops 2048 | bytes 33280 | tf_op jit(solution)/shard_map/scatter-add | solution.py:122
  291.9 3.2 fusion.9
  295.3 2.7 copy.192
  298.0 10.4 %gather_fusion.4 = f32[1024,5,8]{2,1,0:T(8,128)} fusion(f32[5,8,1024]{1,0,2:T(8,128)} %copy.192, s32[1024]{0:T(1024)S(1)} %fusion.60), kind=kCustom, calls=%fused_computation.4.clone | custom fusion | bytes 331776 | tf_op jit(solution)/shard_map/jit(_take)/gather | solution.py:141
  308.3 10.3 %gather_fusion.5 = f32[1024,5,8]{2,1,0:T(8,128)} fusion(f32[5,8,1024]{1,0,2:T(8,128)} %copy.192, s32[1024]{0:T(1024)S(1)} %fusion.61), kind=kCustom, calls=%fused_computation.5.clone | custom fusion | bytes 331776 | tf_op jit(solution)/shard_map/jit(_take)/gather | solution.py:140
  318.6 10.4 %gather_fusion.6 = f32[1024,5,8]{2,1,0:T(8,128)} fusion(f32[5,8,1024]{1,0,2:T(8,128)} %copy.192, s32[1024]{0:T(1024)S(1)} %fusion.62), kind=kCustom, calls=%fused_computation.6.clone | custom fusion | bytes 331776 | tf_op jit(solution)/shard_map/jit(_take)/gather | solution.py:139
  329.0 10.4 %gather_fusion.7 = f32[1024,5,8]{2,1,0:T(8,128)} fusion(f32[5,8,1024]{1,0,2:T(8,128)} %copy.192, s32[1024]{0:T(1024)S(1)} %fusion.63), kind=kCustom, calls=%fused_computation.7.clone | custom fusion | bytes 331776 | tf_op jit(solution)/shard_map/jit(_take)/gather | solution.py:138
  344.7 2.6 copy.197
  353.7 38.4 %all-gather.8.cloned.1.call-done = f32[5,64,1024]{2,1,0:T(8,128)} async-done(((f32[5,8,1024]{2,1,0:T(8,128)}), f32[5,64,1024]{2,1,0:T(8,128)}) %all-gather.8.cloned.1.call-update) | async-done | bytes 1310736 | tf_op jit(solution)/shard_map/all_gather | solution.py:146
  392.1 3.2 fusion.7
  395.5 2.7 copy.200
  398.1 10.4 %gather_fusion.8 = f32[1024,5,8]{2,1,0:T(8,128)} fusion(f32[5,8,1024]{1,0,2:T(8,128)} %copy.200, s32[1024]{0:T(1024)S(1)} %fusion.60), kind=kCustom, calls=%fused_computation.8.clone | custom fusion | bytes 331776 | tf_op jit(solution)/shard_map/jit(_take)/gather | solution.py:141
  408.5 10.3 %gather_fusion.9 = f32[1024,5,8]{2,1,0:T(8,128)} fusion(f32[5,8,1024]{1,0,2:T(8,128)} %copy.200, s32[1024]{0:T(1024)S(1)} %fusion.61), kind=kCustom, calls=%fused_computation.9.clone | custom fusion | bytes 331776 | tf_op jit(solution)/shard_map/jit(_take)/gather | solution.py:140
  418.8 10.4 %gather_fusion.10 = f32[1024,5,8]{2,1,0:T(8,128)} fusion(f32[5,8,1024]{1,0,2:T(8,128)} %copy.200, s32[1024]{0:T(1024)S(1)} %fusion.62), kind=kCustom, calls=%fused_computation.10.clone | custom fusion | bytes 331776 | tf_op jit(solution)/shard_map/jit(_take)/gather | solution.py:139
  429.2 10.4 %gather_fusion.11 = f32[1024,5,8]{2,1,0:T(8,128)} fusion(f32[5,8,1024]{1,0,2:T(8,128)} %copy.200, s32[1024]{0:T(1024)S(1)} %fusion.63), kind=kCustom, calls=%fused_computation.11.clone | custom fusion | bytes 331776 | tf_op jit(solution)/shard_map/jit(_take)/gather | solution.py:138
  450.1 3.0 collective-permute-start.4
  454.0 2.9 collective-permute-done.5
  457.2 35.7 %all-gather.10.cloned.1.call-done = f32[5,64,1024]{2,1,0:T(8,128)} async-done(((f32[5,8,1024]{2,1,0:T(8,128)}), f32[5,64,1024]{2,1,0:T(8,128)}) %all-gather.10.cloned.1.call-update) | async-done | bytes 1310736 | tf_op jit(solution)/shard_map/all_gather | solution.py:146
  492.9 3.2 fusion.5
  (121 shorter events, 56.8 us)
Async XLA Ops:
  7.4 272.1 %all-reduce.80.cloned.1.call-start = ((), (), s32[]{:S(2)}) async-start(), calls=%async_computation.1 | async-start | bytes 2097152 | tf_op jit(solution)/shard_map/psum | solution.py:117
  8.0 42.7 %copy-start.4 = (f32[5,1,8,1024]{3,2,1,0:T(8,128)S(1)}, f32[5,1,8,1024]{3,2,1,0:T(8,128)}, u32[]{:S(2)}) copy-start(f32[5,1,8,1024]{3,2,1,0:T(8,128)} %param.15) | copy-start | bytes 491524
  46.1 7.2 %copy-start.9 = (s32[4,1024]{1,0:T(4,128)S(1)}, s32[4,1024]{1,0:T(4,128)}, u32[]{:S(2)}) copy-start(s32[4,1024]{1,0:T(4,128)} %param.25) | copy-start | bytes 49156
  46.2 245.8 %all-gather.6.cloned.1.call-start = ((), (), s32[]{:S(2)}) async-start(), calls=%async_computation | async-start | bytes 1474560 | tf_op jit(solution)/shard_map/all_gather | solution.py:146
  47.3 58.6 %collective-permute-start = (f32[5,1,1024]{2,1,0:T(1,128)S(1)}, f32[5,1,1024]{2,1,0:T(1,128)S(1)}, u32[]{:S(2)}, u32[]{:S(2)}) collective-permute-start(f32[5,1,1024]{2,1,0:T(1,128)S(1)} %get-tuple-element.160), channel_id=1, source_target_pairs={{0,1},{1,2},{2,3},{3,4},{4,5},{5,6},{6,7},{7,8},{8,9},{9,10},{10,1... | collective-permute-start | bytes 61448 | tf_op jit(solution)/shard_map/ppermute | solution.py:27
  50.0 55.9 %collective-permute-start.1 = (f32[5,1,1024]{2,1,0:T(1,128)S(1)}, f32[5,1,1024]{2,1,0:T(1,128)S(1)}, u32[]{:S(2)}, u32[]{:S(2)}) collective-permute-start(f32[5,1,1024]{2,1,0:T(1,128)S(1)} %get-tuple-element.159), channel_id=1, source_target_pairs={{1,0},{2,1},{3,2},{4,3},{5,4},{6,5},{7,6},{8,7},{9,8},{10,9},{11,1... | collective-permute-start | bytes 61448 | tf_op jit(solution)/shard_map/ppermute | solution.py:29
  50.7 341.5 %all-gather.8.cloned.1.call-start = ((), (), s32[]{:S(2)}) async-start(), calls=%async_computation.2 | async-start | bytes 1474560 | tf_op jit(solution)/shard_map/all_gather | solution.py:146
  89.9 15.8 %copy-start.5 = (f32[1,8,1024]{2,1,0:T(8,128)S(1)}, f32[1,8,1024]{2,1,0:T(8,128)}, u32[]{:S(2)}) copy-start(f32[1,8,1024]{2,1,0:T(8,128)} %param.16) | copy-start | bytes 98308
  89.9 15.8 %copy-start.6 = (f32[3,1,8,1024]{3,2,1,0:T(8,128)S(1)}, f32[3,1,8,1024]{3,2,1,0:T(8,128)}, u32[]{:S(2)}) copy-start(f32[3,1,8,1024]{3,2,1,0:T(8,128)} %param.17) | copy-start | bytes 294916
  89.9 15.9 %copy-start.7 = (f32[1,8,1024]{2,1,0:T(8,128)S(1)}, f32[1,8,1024]{2,1,0:T(8,128)}, u32[]{:S(2)}) copy-start(f32[1,8,1024]{2,1,0:T(8,128)} %param.18) | copy-start | bytes 98308
  103.0 3.0 copy-start.10
  103.0 176.4 %copy-start.8 = (f32[3,2048]{1,0:T(4,128)S(1)}, f32[3,2048]{1,0:T(4,128)}, u32[]{:S(2)}) copy-start(f32[3,2048]{1,0:T(4,128)} %param.23) | copy-start | bytes 73732
  295.3 44.1 %copy-start.2 = (f32[5,8,1024]{2,1,0:T(8,128)}, f32[5,8,1024]{2,1,0:T(8,128)S(1)}, u32[]{:S(2)}) copy-start(f32[5,8,1024]{2,1,0:T(8,128)S(1)} %fusion.36) | copy-start | bytes 491524
  339.5 153.5 %all-gather.10.cloned.1.call-start = ((), (), s32[]{:S(2)}) async-start(), calls=%async_computation.3 | async-start | bytes 1474560 | tf_op jit(solution)/shard_map/all_gather | solution.py:146
  344.7 5.2 %copy-start.3 = (f32[5,8,1024]{2,1,0:T(8,128)S(1)}, f32[5,8,1024]{2,1,0:T(8,128)}, u32[]{:S(2)}) copy-start(f32[5,8,1024]{2,1,0:T(8,128)} %copy-done.2) | copy-start | bytes 491524
  350.0 1.3 collective-permute-start.2
  350.1 3.3 collective-permute-start.3
  395.5 44.1 %copy-start = (f32[5,8,1024]{2,1,0:T(8,128)}, f32[5,8,1024]{2,1,0:T(8,128)S(1)}, u32[]{:S(2)}) copy-start(f32[5,8,1024]{2,1,0:T(8,128)S(1)} %fusion.25) | copy-start | bytes 491524
  444.8 5.2 %copy-start.1 = (f32[5,8,1024]{2,1,0:T(8,128)S(1)}, f32[5,8,1024]{2,1,0:T(8,128)}, u32[]{:S(2)}) copy-start(f32[5,8,1024]{2,1,0:T(8,128)} %copy-done) | copy-start | bytes 491524
  450.1 3.9 collective-permute-start.4
  453.1 3.8 collective-permute-start.5
Sparse Core Ops, SparseCore 0:
  46.3 233.1 all-reduce.79
Sparse Core Ops, SparseCore 1:
  50.7 57.1 all-gather.5
  339.5 52.5 all-gather.7
  439.7 53.2 all-gather.9
where the time goes:
time: 506 us; the launch traced here: 505 us
  waiting for transfers between devices  254 us (50%)
  local copies, waits for them, and re-layouts  175 us (35%)
  other arithmetic  43.5 us (9%)
  between operations  15.5 us (3%)
  matrix products  9.46 us (2%)
  starting transfers between devices  7.07 us (1%)
    psum x1, waiting for transfers between devices, shards(): total = lax.psum(whole, 'space')  173 us
    all_gather x3, waiting for transfers between devices, shards(): every_instant = lax.all_gather(psi[:, None], 'inst', axis=1, tiled=True)  74.2 us
    gather x6, local copies, waits for them, and re-layouts, shards(): minus_y = jnp.take(psi, plane_nbr[1], axis=2)  39.2 us
    gather x6, local copies, waits for them, and re-layouts, shards(): plus_y = jnp.take(psi, plane_nbr[0], axis=2)  39 us
    gather x6, local copies, waits for them, and re-layouts, shards(): minus_z = jnp.take(psi, plane_nbr[3], axis=2)  38.9 us
    gather x6, local copies, waits for them, and re-layouts, shards(): plus_z = jnp.take(psi, plane_nbr[2], axis=2)  38.9 us
    div x4, other arithmetic, panel_block(): (observers[3][:, None] * jnp.cos(phase) + observers[4][:, None] * jnp.sin...  17.3 us
    scatter-add x1, other arithmetic, shards(): jax.ops.segment_sum(weight, panel_cell, num_segments=layers * plane)  11.6 us
  transfers between devices with their start and end apart: 10, of which 7 were waited for; matrix products, arithmetic and copies ran while one was open for 18% of the time, Pallas kernels for 0%

commit v1 on v0

--- a/solution.py
+++ b/solution.py
@@ -92,6 +92,23 @@
     return jnp.where(offset == 0, VISCO * OMEGA * OMEGA * (count * count + 2.0) / 12.0, other)
 
 
+def split_three(values):
+    high = lax.reduce_precision(values, exponent_bits=8, mantissa_bits=7)
+    rest = values - high
+    middle = lax.reduce_precision(rest, exponent_bits=8, mantissa_bits=7)
+    low = rest - middle
+    return jnp.stack([high, middle, low]).astype(jnp.bfloat16)
+
+
+def plane_gather(psi, onehot):
+    comps, layers, plane = psi.shape
+    parts = split_three(psi.reshape(comps * layers, plane))
+    picked = jnp.einsum("pra,kba->kprb", parts, onehot,
+                        preferred_element_type=jnp.float32)
+    picked = (picked[:, 0] + picked[:, 1]) + picked[:, 2]
+    return picked.reshape(onehot.shape[0], comps, layers, plane)
+
+
 def shards(
     psi_start,
     density,
@@ -108,15 +125,25 @@
     inst_count = lax.axis_size("inst")
     inst_id = lax.axis_index("inst")
     space_id = lax.axis_index("space")
-    time_now = 2.0 * math.pi * inst_id.astype(jnp.float32) / inst_count
-    observers = jnp.concatenate(
+    times = jnp.array([2.0 * math.pi * i / inst_count for i in range(inst_count)], jnp.float32)
+    time_now = times[inst_id]
+    local_obs = jnp.concatenate(
         [obs_pos, obs_weight, obs_harmonic[None].astype(jnp.float32)], axis=0
     )
+    observers = lax.all_gather(local_obs, "space", axis=1, tiled=True)
     owned_count = panel_normal.shape[1]
-    whole = sensitivity(observers, panel_pos, time_now)
-    total = lax.psum(whole, "space")
-    sens = lax.dynamic_slice_in_dim(total, space_id * owned_count, owned_count, 1)
-    weight = jnp.sum(sens * panel_normal, axis=0)
+    mine = lax.dynamic_slice_in_dim(panel_pos, space_id * owned_count, owned_count, 1)
+    delta = mine[:, None, :] - observers[:3, :, None]
+    dist2 = jnp.sum(delta * delta, axis=0)
+    dist = jnp.sqrt(dist2)
+    phase = observers[5][:, None] * (time_now - KWAVE * dist)
+    amp = (
+        (observers[3][:, None] * jnp.cos(phase) + observers[4][:, None] * jnp.sin(phase))
+        * (RADIUS * RADIUS)
+        / (dist2 * dist)
+    )
+    along = jnp.sum(delta * panel_normal[:, None, :], axis=0)
+    weight = jnp.sum(amp * along, axis=0)
     layers = psi_start.shape[2]
     plane = psi_start.shape[3]
     wall = jax.ops.segment_sum(weight, panel_cell, num_segments=layers * plane).reshape(
@@ -130,24 +157,24 @@
     ) * (GAMMA - 1.0)
     source = slope * wall[None]
     _, pull = jax.vjp(fluxes, state)
+    onehot = (plane_nbr[:, :, None] == jnp.arange(plane, dtype=jnp.int32)[None, None, :]).astype(
+        jnp.bfloat16
+    )
+    others = jnp.arange(inst_count, dtype=jnp.int32)
+    row_entry = spectral_coeff(
+        jnp.mod(inst_id - others, inst_count).astype(jnp.float32), float(inst_count)
+    )
     psi = psi_start[:, 0]
     for step in range(ITERS):
         padded = padded_2(psi, (("space", 1),), 1)
         minus_a = padded[:, :-2]
         plus_a = padded[:, 2:]
-        plus_y = jnp.take(psi, plane_nbr[0], axis=2)
-        minus_y = jnp.take(psi, plane_nbr[1], axis=2)
-        plus_z = jnp.take(psi, plane_nbr[2], axis=2)
-        minus_z = jnp.take(psi, plane_nbr[3], axis=2)
+        plus_y, minus_y, plus_z, minus_z = plane_gather(psi, onehot)
         middle_point = pull(
             (0.5 * (minus_a - plus_a), 0.5 * (minus_y - plus_y), 0.5 * (minus_z - plus_z))
         )[0]
         spread = 6.0 * psi - (minus_a + plus_a + plus_y + minus_y + plus_z + minus_z)
         every_instant = lax.all_gather(psi[:, None], "inst", axis=1, tiled=True)
-        others = jnp.arange(inst_count, dtype=jnp.int32)
-        row_entry = spectral_coeff(
-            jnp.mod(inst_id - others, inst_count).astype(jnp.float32), float(inst_count)
-        )
         spectral_operator = jnp.einsum(
             "c,kcyo->kyo", row_entry, every_instant, precision=lax.Precision.HIGHEST
         )

time: 506 us -> 219 us (0.43)
  waiting for transfers between devices: 254 us -> 85 us
  local copies, waits for them, and re-layouts: 175 us -> 6.47 us
  blocking collectives: 0 us -> 36.2 us
  matrix products: 9.46 us -> 20.1 us
  other arithmetic: 43.5 us -> 48.8 us
    psum x1 -> x0, waiting for transfers between devices: 173 us -> none  [shards(): total = lax.psum(whole, 'space')]
    gather x24 -> x0, local copies, waits for them, and re-layouts: 156 us -> none  [the longest x6 39.2 us: shards(): minus_y = jnp.take(psi, plane_nbr[1], axis=2)]
    all_gather x0 -> x1, blocking collectives: none -> 36.2 us  [shards(): observers = lax.all_gather(local_obs, 'space', axis=1, tiled=True)]
    div x4 -> x1, other arithmetic: 17.3 us -> 0.94 us  [fluxes(): vel = moment / dens]
    reduce_sum x9 -> x2, other arithmetic: 11.5 us -> 27.3 us  [the longest x1 19.1 us: shards(): weight = jnp.sum(amp * along, axis=0)]
    dot_general x0 -> x3, matrix products: none -> 10.7 us  [plane_gather(): jnp.einsum('pra,kba->kprb', parts, onehot, preferred_element_type=jnp.flo...]
    all_gather x3, waiting for transfers between devices: 74.2 us -> 84.2 us  [shards(): every_instant = lax.all_gather(psi[:, None], 'inst', axis=1, tiled=True)]
    sub x6 -> x0, local copies, waits for them, and re-layouts: 9.33 us -> none  [the longest x2 5.31 us: shards(): psi - TAU * (middle_point + DISSIP * spread + spectral_operator + source)]
  transfers between devices with their start and end apart: 10 -> 9, of which waited for: 7 -> 2; matrix products, arithmetic and copies ran while one was open for 18% -> 28% of each run, Pallas kernels for 0% -> 0%
where the time goes in v1:
time: 219 us; the launch traced here: 218 us
  waiting for transfers between devices  85 us (39%)
  other arithmetic  48.8 us (22%)
  blocking collectives  36.2 us (17%)
  matrix products  20.1 us (9%)
  between operations  13.6 us (6%)
  starting transfers between devices  7.98 us (4%)
  local copies, waits for them, and re-layouts  6.47 us (3%)
    all_gather x3, waiting for transfers between devices, shards(): every_instant = lax.all_gather(psi[:, None], 'inst', axis=1, tiled=True)  84.2 us
    all_gather x1, blocking collectives, shards(): observers = lax.all_gather(local_obs, 'space', axis=1, tiled=True)  36.2 us
    reduce_sum x1, other arithmetic, shards(): weight = jnp.sum(amp * along, axis=0)  19.1 us
    scatter-add x1, other arithmetic, shards(): jax.ops.segment_sum(weight, panel_cell, num_segments=layers * plane)  11.6 us
    dot_general x3, matrix products, plane_gather(): jnp.einsum('pra,kba->kprb', parts, onehot, preferred_element_type=jnp.flo...  10.7 us
    dot_general x3, matrix products, shards(): jnp.einsum('c,kcyo->kyo', row_entry, every_instant, precision=lax.Precisi...  9.47 us
    reduce_sum x1, other arithmetic, shards(): dist2 = jnp.sum(delta * delta, axis=0)  8.23 us
    another operation x5, other arithmetic  4.53 us
  transfers between devices with their start and end apart: 9, of which 2 were waited for; matrix products, arithmetic and copies ran while one was open for 28% of the time, Pallas kernels for 0%

profile of v1, /device:TPU:1, one launch (start us, length us, event | category | flops | bytes accessed | tf_op | source)
XLA Modules:
  0.0 218.1 jit_solution(7759473226278861081)
XLA Ops:
  6.5 0.7 all-gather.7.cloned.1.call-update
  7.3 1.0 fusion.115
  8.3 3.3 %collective-permute-start.1 = (f32[5,1,1024]{2,1,0:T(1,128)S(1)}, f32[5,1,1024]{2,1,0:T(1,128)S(1)}, u32[]{:S(2)}, u32[]{:S(2)}) collective-permute-start(f32[5,1,1024]{2,1,0:T(1,128)S(1)} %get-tuple-element.121), channel_id=1, source_target_pairs={{1,0},{2,1},{3,2},{4,3},{5,4},{6,5},{7,6},{8,7},{9,8},{10,9},{11,1... | collective-permute-start | bytes 61448 | tf_op jit(solution)/shard_map/ppermute | solution.py:29
  11.6 0.7 convert_bitcast_fusion
  12.3 0.7 maximum_bitcast_fusion.6
  13.0 36.2 %all-gather.2 = f32[32,16,6]{1,2,0:T(8,128)S(1)} all-gather(f32[1,16,6]{1,2,0:T(8,128)S(1)} %maximum_bitcast_fusion.6), channel_id=1, replica_groups=mesh['inst'=8,'space'=32] {'space'}, dimensions={0}, use_global_device_ids=true | all-gather | bytes 12672 | tf_op jit(solution)/shard_map/all_gather | solution.py:133
  49.3 1.0 reduce-precision_convert_fusion.5
  50.3 0.9 broadcast_divide_fusion
  51.2 0.8 multiply_reduce_fusion.3
  52.1 1.2 dynamic_slice.6
  53.3 8.2 %fusion.7 = (f32[512,2048]{1,0:T(8,128)S(1)}, f32[512,2048]{1,0:T(8,128)S(1)}) fusion(f32[3,512]{1,0:T(4,128)S(1)} %slice.195, f32[3,2048]{1,0:T(4,128)S(1)} %constant_dynamic-slice_fusion, f32[3,2048]{1,0:T(4,128)} %param.20), kind=kLoop, calls=%fused_computation.8 | loop fusion | flops 13631488 | bytes 8443904 | tf_op jit(solution)/shard_map/reduce_sum | solution.py:137
  61.5 19.1 %fusion.16 = f32[2048]{0:T(1024)S(1)} fusion(f32[512,2048]{1,0:T(8,128)S(1)} %get-tuple-element.6, f32[512,2048]{1,0:T(8,128)S(1)} %get-tuple-element.5, f32[512]{0:T(512)S(1)} %bitcast.236, f32[]{:T(128)} %bitcast.26, f32[512]{0:T(512)S(1)} %bitcast.237, f32[512]{0:T(512)S(1)} %bitcast.235), kind=kLoop, calls=%fused_computation.19 | loop fusion | flops 11532288 | bytes 8402948 | tf_op jit(solution)/shard_map/reduce_sum | solution.py:146
  80.7 11.6 %scatter_custom_fusion = f32[8192]{0:T(1024)S(1)} fusion(s32[2048]{0:T(1024)} %param.21, f32[2048]{0:T(1024)S(1)} %fusion.16, f32[]{:T(128)} %constant.27.clone.1), kind=kCustom, calls=%fused_computation.222 | custom fusion | flops 2048 | bytes 33280 | tf_op jit(solution)/shard_map/scatter-add | solution.py:149
  92.3 3.6 %fusion.17 = f32[4,3,40,1024]{3,2,1,0:T(8,128)S(1)} fusion(s32[4,1024]{1,0:T(4,128)S(1)} %copy-done.7, bf16[1,40,1024]{2,1,0:T(8,128)(2,1)S(1)} %get-tuple-element.123, bf16[1,40,1024]{2,1,0:T(8,128)(2,1)S(1)} %get-tuple-element.124, bf16[1,40,1024]{2,1,0:T(8,128)(2,1)S(1)} %get-tuple-element.122), kind=kOutput, calls=%fused_computation.20 | convolution fusion | flops 1011564544 | bytes 2228224 | tf_op jit(solution)/shard_map/pra,kba->kprb/dot_general | solution.py:106
  97.1 3.2 %fusion.30 = f32[1,5,8,1024]{3,0,2,1:T(1,128)S(1)} fusion(f32[5,8,8,1024]{3,2,1,0:T(8,128)} %all-gather.7.cloned.1.call-done, s32[]{:T(128)S(6)} %axis_index.23), kind=kOutput, calls=%fused_computation.27 | convolution fusion | flops 3932416 | bytes 1474564 | tf_op jit(solution)/shard_map/c,kcyo->kyo/dot_general | solution.py:178
  100.3 0.8 reduce-precision_convert_fusion.3
  101.2 1.0 reduce-precision_convert_fusion.2
  102.2 1.0 fusion.114
  103.4 1.6 collective-permute-start.2
  105.0 3.6 %fusion.20 = f32[4,3,40,1024]{3,2,1,0:T(8,128)S(1)} fusion(s32[4,1024]{1,0:T(4,128)S(1)} %copy-done.7, bf16[1,40,1024]{2,1,0:T(8,128)(2,1)S(1)} %get-tuple-element.109, bf16[1,40,1024]{2,1,0:T(8,128)(2,1)S(1)} %get-tuple-element.108, bf16[1,40,1024]{2,1,0:T(8,128)(2,1)S(1)} %get-tuple-element.17), kind=kOutput, calls=%fused_computation.21 | convolution fusion | flops 1011564544 | bytes 2228224 | tf_op jit(solution)/shard_map/pra,kba->kprb/dot_general | solution.py:106
  108.8 0.7 copy-done.2
  109.8 40.8 %all-gather.9.cloned.1.call-done = f32[5,64,1024]{2,1,0:T(8,128)} async-done(((f32[5,8,1024]{2,1,0:T(8,128)}), f32[5,64,1024]{2,1,0:T(8,128)}) %all-gather.9.cloned.1.call-update) | async-done | bytes 1310736 | tf_op jit(solution)/shard_map/all_gather | solution.py:177
  150.6 3.2 %fusion.28 = f32[1,5,8,1024]{3,0,2,1:T(1,128)S(1)} fusion(f32[5,8,8,1024]{3,2,1,0:T(8,128)} %bitcast.227, s32[]{:T(128)S(6)} %axis_index.23), kind=kOutput, calls=%fused_computation.25 | convolution fusion | flops 3932416 | bytes 1474564 | tf_op jit(solution)/shard_map/c,kcyo->kyo/dot_general | solution.py:178
  153.7 0.8 reduce-precision_convert_fusion.1
  154.6 1.0 fusion.113
  155.6 1.0 reduce-precision_convert_fusion
  156.6 2.6 %collective-permute-start.4 = (f32[5,1,1024]{2,1,0:T(1,128)S(1)}, f32[5,1,1024]{2,1,0:T(1,128)S(1)}, u32[]{:S(2)}, u32[]{:S(2)}) collective-permute-start(f32[5,1,1024]{2,1,0:T(1,128)S(1)} %get-tuple-element.96), channel_id=1, source_target_pairs={{0,1},{1,2},{2,3},{3,4},{4,5},{5,6},{6,7},{7,8},{8,9},{9,10},{10,1... | collective-permute-start | bytes 61448 | tf_op jit(solution)/shard_map/ppermute | solution.py:27
  159.4 3.6 %fusion.23 = f32[4,3,40,1024]{3,2,1,0:T(8,128)S(1)} fusion(s32[4,1024]{1,0:T(4,128)S(1)} %copy-done.7, bf16[1,40,1024]{2,1,0:T(8,128)(2,1)S(1)} %get-tuple-element.94, bf16[1,40,1024]{2,1,0:T(8,128)(2,1)S(1)} %get-tuple-element.93, bf16[1,40,1024]{2,1,0:T(8,128)(2,1)S(1)} %get-tuple-element.11), kind=kOutput, calls=%fused_computation.22 | convolution fusion | flops 1011564544 | bytes 2228224 | tf_op jit(solution)/shard_map/pra,kba->kprb/dot_general | solution.py:106
  163.2 0.7 copy-done.1
  164.2 43.5 %all-gather.11.cloned.1.call-done = f32[5,64,1024]{2,1,0:T(8,128)} async-done(((f32[5,8,1024]{2,1,0:T(8,128)}), f32[5,64,1024]{2,1,0:T(8,128)}) %all-gather.11.cloned.1.call-update) | async-done | bytes 1310736 | tf_op jit(solution)/shard_map/all_gather | solution.py:177
  207.6 3.2 %fusion.26 = f32[1,5,8,1024]{3,0,2,1:T(1,128)S(1)} fusion(f32[5,8,8,1024]{3,2,1,0:T(8,128)} %bitcast.226, s32[]{:T(128)S(6)} %axis_index.23), kind=kOutput, calls=%fused_computation.23 | convolution fusion | flops 3932416 | bytes 1474564 | tf_op jit(solution)/shard_map/c,kcyo->kyo/dot_general | solution.py:178
  210.8 0.8 fusion.50
  (67 shorter events, 2.8 us)
Async XLA Ops:
  6.5 45.5 %copy-start = (f32[3,65536]{1,0:T(4,128)S(1)}, f32[3,65536]{1,0:T(4,128)}, u32[]{:S(2)}) copy-start(f32[3,65536]{1,0:T(4,128)} %param.19) | copy-start | bytes 2359300
  6.5 90.6 %all-gather.7.cloned.1.call-start = ((), (), s32[]{:S(2)}) async-start(), calls=%async_computation | async-start | bytes 1474560 | tf_op jit(solution)/shard_map/all_gather | solution.py:177
  7.3 143.3 %all-gather.9.cloned.1.call-start = ((), (), s32[]{:S(2)}) async-start(), calls=%async_computation.1 | async-start | bytes 1474560 | tf_op jit(solution)/shard_map/all_gather | solution.py:177
  8.3 87.8 %collective-permute-start.1 = (f32[5,1,1024]{2,1,0:T(1,128)S(1)}, f32[5,1,1024]{2,1,0:T(1,128)S(1)}, u32[]{:S(2)}, u32[]{:S(2)}) collective-permute-start(f32[5,1,1024]{2,1,0:T(1,128)S(1)} %get-tuple-element.121), channel_id=1, source_target_pairs={{1,0},{2,1},{3,2},{4,3},{5,4},{6,5},{7,6},{8,7},{9,8},{10,9},{11,1... | collective-permute-start | bytes 61448 | tf_op jit(solution)/shard_map/ppermute | solution.py:29
  11.6 84.5 %collective-permute-start = (f32[5,1,1024]{2,1,0:T(1,128)S(1)}, f32[5,1,1024]{2,1,0:T(1,128)S(1)}, u32[]{:S(2)}, u32[]{:S(2)}) collective-permute-start(f32[5,1,1024]{2,1,0:T(1,128)S(1)} %get-tuple-element.120), channel_id=1, source_target_pairs={{0,1},{1,2},{2,3},{3,4},{4,5},{5,6},{6,7},{7,8},{8,9},{9,10},{10,1... | collective-permute-start | bytes 61448 | tf_op jit(solution)/shard_map/ppermute | solution.py:27
  61.5 30.7 %copy-start.7 = (s32[4,1024]{1,0:T(4,128)S(1)}, s32[4,1024]{1,0:T(4,128)}, u32[]{:S(2)}) copy-start(s32[4,1024]{1,0:T(4,128)} %param.22) | copy-start | bytes 49156
  92.3 3.8 %copy-start.4 = (f32[1,8,1024]{2,1,0:T(8,128)S(1)}, f32[1,8,1024]{2,1,0:T(8,128)}, u32[]{:S(2)}) copy-start(f32[1,8,1024]{2,1,0:T(8,128)} %param.13) | copy-start | bytes 98308
  92.3 3.8 %copy-start.5 = (f32[1,8,1024]{2,1,0:T(8,128)S(1)}, f32[1,8,1024]{2,1,0:T(8,128)}, u32[]{:S(2)}) copy-start(f32[1,8,1024]{2,1,0:T(8,128)} %param.15) | copy-start | bytes 98308
  95.8 0.9 copy-start.3
  95.9 1.1 copy-start.6
  101.2 106.5 %all-gather.11.cloned.1.call-start = ((), (), s32[]{:S(2)}) async-start(), calls=%async_computation.2 | async-start | bytes 1474560 | tf_op jit(solution)/shard_map/all_gather | solution.py:177
  103.2 5.6 %collective-permute-start.3 = (f32[5,1,1024]{2,1,0:T(1,128)S(1)}, f32[5,1,1024]{2,1,0:T(1,128)S(1)}, u32[]{:S(2)}, u32[]{:S(2)}) collective-permute-start(f32[5,1,1024]{2,1,0:T(1,128)S(1)} %get-tuple-element.107), channel_id=1, source_target_pairs={{1,0},{2,1},{3,2},{4,3},{5,4},{6,5},{7,6},{8,7},{9,8},{10,9},{11,1... | collective-permute-start | bytes 61448 | tf_op jit(solution)/shard_map/ppermute | solution.py:29
  103.4 5.4 %collective-permute-start.2 = (f32[5,1,1024]{2,1,0:T(1,128)S(1)}, f32[5,1,1024]{2,1,0:T(1,128)S(1)}, u32[]{:S(2)}, u32[]{:S(2)}) collective-permute-start(f32[5,1,1024]{2,1,0:T(1,128)S(1)} %get-tuple-element.106), channel_id=1, source_target_pairs={{0,1},{1,2},{2,3},{3,4},{4,5},{5,6},{6,7},{7,8},{8,9},{9,10},{10,1... | collective-permute-start | bytes 61448 | tf_op jit(solution)/shard_map/ppermute | solution.py:27
  108.6 0.9 copy-start.2
  156.6 6.6 %collective-permute-start.4 = (f32[5,1,1024]{2,1,0:T(1,128)S(1)}, f32[5,1,1024]{2,1,0:T(1,128)S(1)}, u32[]{:S(2)}, u32[]{:S(2)}) collective-permute-start(f32[5,1,1024]{2,1,0:T(1,128)S(1)} %get-tuple-element.96), channel_id=1, source_target_pairs={{0,1},{1,2},{2,3},{3,4},{4,5},{5,6},{6,7},{7,8},{8,9},{9,10},{10,1... | collective-permute-start | bytes 61448 | tf_op jit(solution)/shard_map/ppermute | solution.py:27
  159.2 4.0 %collective-permute-start.5 = (f32[5,1,1024]{2,1,0:T(1,128)S(1)}, f32[5,1,1024]{2,1,0:T(1,128)S(1)}, u32[]{:S(2)}, u32[]{:S(2)}) collective-permute-start(f32[5,1,1024]{2,1,0:T(1,128)S(1)} %get-tuple-element.95), channel_id=1, source_target_pairs={{1,0},{2,1},{3,2},{4,3},{5,4},{6,5},{7,6},{8,7},{9,8},{10,9},{11,1... | collective-permute-start | bytes 61448 | tf_op jit(solution)/shard_map/ppermute | solution.py:29
  162.9 0.9 copy-start.1
Sparse Core Ops, SparseCore 0:
  10.0 56.1 all-gather.6
  101.3 49.2 all-gather.8
  154.7 52.8 all-gather.10
